TPU v7x, 32 devices: a whole 2x2x4 slice. The times are simulated.
32 devices in a mesh: dp: 2 (over x), hist: 16 (over z, y, core).
Axes of the slice: x: 2, y: 2, z: 4, core: 2. Of those that a mesh axis runs over, the one named last changes fastest.
Arguments:
- queries: bfloat16 [2, 8192, 512], P('dp', 'hist'), may hold values from -6 to 6
- key_rows: bfloat16 [2, 8192, 512], P('dp', 'hist'), may hold values from -6 to 6
- value_rows: bfloat16 [2, 8192, 512], P('dp', 'hist'), may hold values from -6 to 6
- gate_rows: bfloat16 [2, 8192, 512], P('dp', 'hist'), may hold values from -6 to 6
- user_start: int32 [2, 8192], P('dp', 'hist'), may hold values from 0 to 8191, as said below
- w_out: bfloat16 [512, 1024], replicated, may hold values from -0.25 to 0.25
- out_grad: bfloat16 [2, 8192, 1024], P('dp', 'hist'), may hold values from -6 to 6
Outputs:
- query_grad: bfloat16 [2, 8192, 512], P('dp', 'hist')
- key_grad: bfloat16 [2, 8192, 512], P('dp', 'hist')
- value_grad: bfloat16 [2, 8192, 512], P('dp', 'hist')
- gate_grad: bfloat16 [2, 8192, 512], P('dp', 'hist')
- weight_grad: float32 [512, 1024], P('hist')
Inputs may be any that keep to these rules, and one draw needn't show every extreme that they name: user_start[g, i] is the position within group g of the first event of event i's user: it is at most i, never falls along the events, equals i where a user begins, and is 0 at the first event; the last event of every group is a user of its own.
All inputs are finite; a program needn't handle non-finite values.
Results may differ from a plain program's by a relative error of at most 0.012.
Values may be sent and summed in bfloat16 or wider, within the bound.
A program may use at most 128 MiB of HBM per device.

v0:
```python
import math
import jax
import jax.numpy as jnp
from jax import lax
from jax.sharding import PartitionSpec as P

HEADS = 4
HS = 128
WIN = 512
EPSILON = 1e-05


def shifted(value, axis, steps):
    count = lax.axis_size(axis)
    first, last = (max(0, -steps), min(count, count - steps))
    return lax.ppermute(value, axis, [(source, source + steps) for source in range(first, last)])


def split_heads(values):
    return values.reshape(values.shape[0], HEADS, HS)


def score_block(query_rows, key_piece):
    product = jnp.einsum(
        "rhd,chd->hrc",
        split_heads(query_rows),
        split_heads(key_piece),
        preferred_element_type=jnp.float32,
    )
    return product * HS ** (-0.5)


def window_mask(query_pos, start_rows, key_pos):
    spacing = query_pos[:, None] - key_pos[None, :]
    return (key_pos[None, :] >= start_rows[:, None]) & (spacing >= 0) & (spacing < WIN)


def silu_weights(scaled, live_map):
    sigmoid_s = jax.nn.sigmoid(scaled)
    weights = jnp.where(live_map[None], scaled * sigmoid_s / WIN, 0.0).astype(jnp.bfloat16)
    return (sigmoid_s, weights)


def attend(query_rows, key_piece, value_piece, live_map):
    scaled = score_block(query_rows, key_piece)
    sigmoid_s, weights = silu_weights(scaled, live_map)
    mixed = jnp.einsum(
        "hrc,chd->rhd", weights, split_heads(value_piece), preferred_element_type=jnp.float32
    )
    return mixed.reshape(query_rows.shape[0], -1)


def back_piece(query_rows, d_attn, key_piece, value_piece, live_map, want_keys):
    inv_root = HS ** (-0.5)
    scaled = score_block(query_rows, key_piece)
    sigmoid_s, weights = silu_weights(scaled, live_map)
    d_weights = jnp.einsum(
        "rhd,chd->hrc",
        split_heads(d_attn),
        split_heads(value_piece),
        preferred_element_type=jnp.float32,
    )
    d_scores = jnp.where(
        live_map[None], d_weights * sigmoid_s * (1.0 + scaled * (1.0 - sigmoid_s)) / WIN, 0.0
    )
    d_scores = d_scores.astype(jnp.bfloat16)
    results = []
    query_part = jnp.einsum(
        "hrc,chd->rhd", d_scores, split_heads(key_piece), preferred_element_type=jnp.float32
    )
    results.append(query_part.reshape(query_rows.shape[0], -1) * inv_root)
    key_part = jnp.einsum(
        "hrc,rhd->chd", d_scores, split_heads(query_rows), preferred_element_type=jnp.float32
    )
    value_part = jnp.einsum(
        "hrc,rhd->chd", weights, split_heads(d_attn), preferred_element_type=jnp.float32
    )
    results.append(key_part.reshape(want_keys, -1) * inv_root)
    results.append(value_part.reshape(want_keys, -1))
    return tuple(results)


def row_section(attended, gate_blk, grad_blk, w_out):
    row_mean = jnp.mean(attended, axis=-1, keepdims=True)
    centred = attended - row_mean
    inverse = lax.rsqrt(jnp.mean(centred * centred, axis=-1, keepdims=True) + EPSILON)
    normed = centred * inverse
    gate_wide = gate_blk.astype(jnp.float32)
    hidden = (normed * gate_wide).astype(jnp.bfloat16)
    d_hidden = lax.dot_general(
        grad_blk, w_out, (((1,), (1,)), ((), ())), preferred_element_type=jnp.float32
    )
    gate_grad = (d_hidden * normed).astype(jnp.bfloat16)
    d_normed = d_hidden * gate_wide
    d_attn = inverse * (
        d_normed
        - jnp.mean(d_normed, axis=-1, keepdims=True)
        - normed * jnp.mean(d_normed * normed, axis=-1, keepdims=True)
    )
    return (hidden, gate_grad, d_attn.astype(jnp.bfloat16))


def shards(queries, key_rows, value_rows, gate_rows, user_start, w_out, out_grad):
    query_loc = queries[0]
    key_loc = key_rows[0]
    value_loc = value_rows[0]
    gate_loc = gate_rows[0]
    start_loc = user_start[0]
    grad_loc = out_grad[0]
    ev_rows = query_loc.shape[0]
    tail = min(WIN, ev_rows)
    reach = -(-WIN // ev_rows)
    index = lax.axis_index("hist")
    hist_size = lax.axis_size("hist")
    row_ids = jnp.arange(ev_rows, dtype=jnp.int32)
    query_pos = index * ev_rows + row_ids
    tail_ids = jnp.arange(tail, dtype=jnp.int32) + (ev_rows - tail)
    offset = 1
    got_keys, got_values = shifted((key_loc, value_loc), "hist", offset)
    halo_pieces = [(got_keys, got_values, (index - offset) * ev_rows + tail_ids)]
    halo_live = [window_mask(query_pos, start_loc, member[2]) for member in halo_pieces]
    local_live = window_mask(query_pos, start_loc, query_pos)
    key_all = jnp.concatenate([member[0] for member in halo_pieces] + [key_loc], 0)
    value_all = jnp.concatenate([member[1] for member in halo_pieces] + [value_loc], 0)
    live_all = jnp.concatenate(halo_live + [local_live], 1)
    attended = attend(query_loc, key_all, value_all, live_all)
    hidden, gate_grad, d_attn = row_section(attended, gate_loc, grad_loc, w_out)
    want_all = reach * tail + ev_rows
    query_part, key_part, value_part = back_piece(
        query_loc, d_attn, key_all, value_all, live_all, want_all
    )
    local_key = key_part[want_all - ev_rows :]
    local_value = value_part[want_all - ev_rows :]
    remote_parts = [(key_part[0:tail], value_part[0:tail])]
    offset = 1
    got_key, got_value = shifted(
        (remote_parts[offset - 1][0], remote_parts[offset - 1][1]), "hist", -offset
    )
    key_total = local_key + got_key
    value_total = local_value + got_value
    weight_part = lax.psum_scatter(
        lax.dot_general(
            hidden, grad_loc, (((0,), (0,)), ((), ())), preferred_element_type=jnp.float32
        ),
        "hist",
        scatter_dimension=0,
        tiled=True,
    )
    weight_total = lax.psum(weight_part.astype(jnp.bfloat16), "dp").astype(jnp.float32)
    total_rows = lax.axis_size("dp") * hist_size * ev_rows
    weight_grad = weight_total / math.sqrt(total_rows)
    return (
        query_part.astype(jnp.bfloat16)[None],
        key_total.astype(jnp.bfloat16)[None],
        value_total.astype(jnp.bfloat16)[None],
        gate_grad[None],
        weight_grad,
    )


def solution(mesh):
    return jax.shard_map(
        shards,
        mesh=mesh,
        in_specs=(
            P("dp", "hist", None),
            P("dp", "hist", None),
            P("dp", "hist", None),
            P("dp", "hist", None),
            P("dp", "hist"),
            P(),
            P("dp", "hist", None),
        ),
        out_specs=(
            P("dp", "hist", None),
            P("dp", "hist", None),
            P("dp", "hist", None),
            P("dp", "hist", None),
            P("hist", None),
        ),
        check_vma=False,
    )
```

profile of v0, /device:TPU:0, one launch (start us, length us, event | category | flops | bytes accessed | tf_op | source)
XLA Modules:
  0.0 138.0 jit_solution(251763052997868147)
XLA Ops:
  7.2 1.4 copy.31
  8.6 3.2 %collective-permute-start = (bf16[512,512]{0,1:T(8,128)(2,1)S(1)}, bf16[512,512]{0,1:T(8,128)(2,1)}, u32[]{:S(2)}, u32[]{:S(2)}) collective-permute-start(bf16[512,512]{0,1:T(8,128)(2,1)S(1)} %bitcast.106), channel_id=1, source_target_pairs={{0,1},{1,2},{2,3},{3,4},{4,5},{5,6},{6,7},{7,8},{8,9},{9,10},{10,1... | collective-permute-start | bytes 1572872 | tf_op jit(solution)/shard_map/ppermute | solution.py:16
  11.8 4.5 %collective-permute-start.1 = (bf16[512,512]{1,0:T(8,128)(2,1)}, bf16[512,512]{1,0:T(8,128)(2,1)}, u32[]{:S(2)}, u32[]{:S(2)}) collective-permute-start(bf16[512,512]{1,0:T(8,128)(2,1)} %bitcast.113), channel_id=1, source_target_pairs={{0,1},{1,2},{2,3},{3,4},{4,5},{5,6},{6,7},{7,8},{8,9},{9,10},{10,1... | collective-permute-start | bytes 1572872 | tf_op jit(solution)/shard_map/ppermute | solution.py:16
  16.4 2.0 %copy.36 = bf16[1,512,512]{1,2,0:T(8,128)(2,1)} copy(bf16[1,512,512]{2,1,0:T(8,128)(2,1)} %param.9) | data formatting | bytes 1048576 | tf_op args[2]
  18.4 1.0 copy.34
  19.4 1.3 copy.62
  21.6 0.8 pad_add_fusion
  22.4 1.3 copy.33
  23.8 7.5 %fusion.5 = (bf16[4,512,1024]{1,2,0:T(8,128)(2,1)}, f32[4,1024,512]{2,1,0:T(8,128)}) fusion(pred[512,1024]{0,1:T(8,128)(4,1)} %pad_add_fusion, bf16[512,4,128]{0,2,1:T(8,128)(2,1)S(1)} %bitcast.111, bf16[512,4,128]{2,0,1:T(8,128)(2,1)} %copy.34, bf16[512,4,128]{2,0,1:T(8,128)(2,1)S(1)} %copy.33), kind=kOutput, calls=%fused_computation.8 | convolution fusion | flops 555745280 | bytes 14680064 | tf_op jit(solution)/shard_map/rhd,chd->hrc/dot_general | solution.py:24
  31.3 2.0 %copy.35 = bf16[512,512]{0,1:T(8,128)(2,1)} copy(bf16[512,512]{1,0:T(8,128)(2,1)} %collective-permute-done.1) | data formatting | bytes 1048576 | tf_op jit(solution)/shard_map/ppermute | solution.py:16
  33.3 3.1 %fusion.32 = (f32[512]{0:T(512)S(1)}, f32[4,128,512]{2,1,0:T(8,128)S(1)}) fusion(bf16[4,512,1024]{1,2,0:T(8,128)(2,1)} %get-tuple-element.25, bf16[512,4,128]{0,2,1:T(8,128)(2,1)S(1)} %bitcast.115, bf16[512,4,128]{0,2,1:T(8,128)(2,1)} %bitcast.116), kind=kOutput, calls=%fused_computation.62 | convolution fusion | flops 539229696 | bytes 6293504 | tf_op jit(solution)/shard_map/hrc,chd->rhd/dot_general | solution.py:47
  36.8 2.0 %fusion.13 = f32[512,1024]{1,0:T(8,128)} fusion(bf16[512,512]{0,1:T(8,128)(2,1)S(1)} %bitcast.108, bf16[1,512,1024]{2,1,0:T(8,128)(2,1)S(1)} %copy-done), kind=kOutput, calls=%fused_computation.28 | convolution fusion | flops 536870912 | bytes 3670016 | tf_op jit(solution)/shard_map/dot_general | solution.py:142
  38.9 2.2 %fusion.25 = (f32[512]{0:T(512)S(1)}, f32[512]{0:T(512)S(1)}, f32[512,512]{0,1:T(8,128)S(1)}) fusion(bf16[1,512,512]{1,2,0:T(8,128)(2,1)S(1)} %copy.39, f32[512]{0:T(512)S(1)} %add_rsqrt_fusion, f32[512]{0:T(512)S(1)} %broadcast_multiply_fusion.2, f32[4,128,512]{2,1,0:T(8,128)S(1)} %get-tuple-element.28, bf16[512,1024]{1,0:T(8,128)(2,1)} %param.12, ...), kind=kOutput, calls=%fused_computation.48 | convolution fusion | flops 538704896 | bytes 4726784 | tf_op jit(solution)/shard_map/dot_general | solution.py:90
  41.2 1.2 multiply_convert_fusion.1
  42.3 1.5 %convolution_bitcast_fusion = f32[1024,4,128]{0,2,1:T(8,128)S(1)} fusion(bf16[512,4,128]{0,2,1:T(8,128)(2,1)S(1)} %bitcast.109, bf16[4,512,1024]{1,2,0:T(8,128)(2,1)S(1)} %copy-done.1), kind=kOutput, calls=%fused_computation.16 | convolution fusion | flops 536870912 | bytes 6815744 | tf_op jit(solution)/shard_map/hrc,rhd->chd/dot_general | solution.py:75
  44.0 1.4 %copy.50 = f32[512,512]{1,0:T(8,128)} copy(f32[512,512]{0,1:T(8,128)S(1)} %bitcast.103) | data formatting | bytes 2097152 | tf_op jit(solution)/shard_map/slice | solution.py:134
  45.5 1.5 %collective-permute-start.3 = (f32[512,512]{1,0:T(8,128)}, f32[512,512]{1,0:T(8,128)}, u32[]{:S(2)}, u32[]{:S(2)}) collective-permute-start(f32[512,512]{1,0:T(8,128)} %copy.50), channel_id=1, source_target_pairs={{1,0},{2,1},{3,2},{4,3},{5,4},{6,5},{7,6},{8,7},{9,8},{10,9},{11,1... | collective-permute-start | bytes 3145736 | tf_op jit(solution)/shard_map/ppermute | solution.py:16
  46.9 7.5 %fusion.10 = bf16[4,512,1024]{1,2,0:T(8,128)(2,1)S(1)} fusion(f32[4,1024,512]{2,1,0:T(8,128)} %get-tuple-element.26, pred[512,1024]{0,1:T(8,128)(4,1)} %pad_add_fusion, bf16[512,4,128]{0,2,1:T(8,128)(2,1)} %bitcast.110, bf16[512,4,128]{0,2,1:T(8,128)(2,1)} %bitcast.114, bf16[512,4,128]{0,2,1:T(8,128)(2,1)} %bitcast.117), kind=kOutput, calls=%fused_computation.13 | convolution fusion | flops 564133888 | bytes 14680064 | tf_op jit(solution)/shard_map/rhd,chd->hrc/dot_general | solution.py:57
  54.5 1.5 %multiply_bitcast_fusion = f32[1024,4,128]{0,2,1:T(8,128)S(1)} fusion(bf16[4,512,1024]{1,2,0:T(8,128)(2,1)S(1)} %fusion.10, bf16[512,4,128]{0,2,1:T(8,128)(2,1)S(1)} %bitcast.112), kind=kOutput, calls=%fused_computation.14 | convolution fusion | flops 537395200 | bytes 6815744 | tf_op jit(solution)/shard_map/hrc,rhd->chd/dot_general | solution.py:72
  56.0 1.1 fusion.31
  57.1 1.3 copy.47
  58.4 1.3 collective-permute-start.2
  60.1 1.6 %copy.48 = f32[512,512]{1,0:T(8,128)S(1)} copy(f32[512,512]{0,1:T(8,128)} %bitcast.102) | data formatting | bytes 2097152 | tf_op jit(solution)/shard_map/slice | solution.py:132
  61.6 4.1 %fusion.11 = bf16[4,128,512]{2,1,0:T(8,128)(2,1)} fusion(bf16[4,512,1024]{1,2,0:T(8,128)(2,1)} %copy-done.2, bf16[512,4,128]{2,0,1:T(8,128)(2,1)} %copy.34, bf16[512,4,128]{2,0,1:T(8,128)(2,1)} %copy-done.8), kind=kOutput, calls=%fused_computation.22 | convolution fusion | flops 539492352 | bytes 5767168 | tf_op jit(solution)/shard_map/hrc,chd->rhd/dot_general | solution.py:68
  65.8 2.1 %copy.52 = bf16[1,512,512]{2,1,0:T(8,128)(2,1)} copy(bf16[1,512,512]{1,2,0:T(8,128)(2,1)} %bitcast.118) | data formatting | bytes 1048576
  67.8 2.0 %copy.53 = bf16[1,512,512]{2,1,0:T(8,128)(2,1)} copy(bf16[1,512,512]{1,2,0:T(8,128)(2,1)} %bitcast.105) | data formatting | bytes 1048576
  69.9 2.2 %fusion.24 = bf16[1,512,512]{2,1,0:T(8,128)(2,1)} fusion(f32[512,512]{1,0:T(8,128)S(1)} %copy.51, f32[512,512]{1,0:T(8,128)} %collective-permute-done.3), kind=kLoop, calls=%fused_computation.47 | loop fusion | flops 524288 | bytes 2621440 | tf_op jit(solution)/shard_map/broadcast_in_dim | solution.py:155
  72.0 34.9 %reduce-scatter.2.cloned.1.call-done = f32[32,1024]{1,0:T(8,128)} async-done(((f32[512,1024]{1,0:T(8,128)}), f32[32,1024]{1,0:T(8,128)}) %reduce-scatter.2.cloned.1.call-update) | async-done | bytes 131088 | tf_op jit(solution)/shard_map/reduce_scatter | solution.py:141
  106.9 1.5 %convert_element_type.74 = bf16[32,1024]{1,0:T(8,128)(2,1)} convert(f32[32,1024]{1,0:T(8,128)} %reduce-scatter.2.cloned.1.call-done) | non-fusion elementwise | flops 32768 | bytes 196608 | tf_op jit(solution)/shard_map/convert_element_type | solution.py:149
  108.5 2.2 %fusion.23 = bf16[1,512,512]{2,1,0:T(8,128)(2,1)} fusion(f32[512,512]{1,0:T(8,128)S(1)} %copy.48, f32[512,512]{1,0:T(8,128)} %collective-permute-done.2), kind=kLoop, calls=%fused_computation.46 | loop fusion | flops 524288 | bytes 2621440 | tf_op jit(solution)/shard_map/broadcast_in_dim | solution.py:154
  110.7 19.0 %all-reduce.2.cloned.1.call-done = bf16[32,1024]{1,0:T(8,128)(2,1)} async-done(((bf16[32,1024]{1,0:T(8,128)(2,1)}), bf16[32,1024]{1,0:T(8,128)(2,1)}) %all-reduce.2.cloned.1.call-update) | async-done | bytes 65552 | tf_op jit(solution)/shard_map/psum | solution.py:149
  129.6 1.5 %convert_multiply_fusion = f32[32,1024]{1,0:T(8,128)} fusion(bf16[32,1024]{1,0:T(8,128)(2,1)} %all-reduce.2.cloned.1.call-done), kind=kLoop, calls=%fused_computation.49 | loop fusion | flops 65536 | bytes 196608 | tf_op jit(solution)/shard_map/div | solution.py:151
  (39 shorter events, 2.0 us)
Async XLA Ops:
  7.2 29.6 %copy-start = (bf16[1,512,1024]{2,1,0:T(8,128)(2,1)S(1)}, bf16[1,512,1024]{2,1,0:T(8,128)(2,1)}, u32[]{:S(2)}) copy-start(bf16[1,512,1024]{2,1,0:T(8,128)(2,1)} %param.13) | copy-start | bytes 3145732
  7.2 13.5 %copy-start.6 = (bf16[1,512,512]{2,1,0:T(8,128)(2,1)S(1)}, bf16[1,512,512]{2,1,0:T(8,128)(2,1)}, u32[]{:S(2)}) copy-start(bf16[1,512,512]{2,1,0:T(8,128)(2,1)} %param.10) | copy-start | bytes 1572868
  7.2 13.7 %copy-start.9 = (s32[1,512]{1,0:T(1,128)S(1)}, s32[1,512]{1,0:T(1,128)}, u32[]{:S(2)}) copy-start(s32[1,512]{1,0:T(1,128)} %param.11) | copy-start | bytes 6148
  7.2 99.7 %reduce-scatter.2.cloned.1.call-start = ((), (), s32[]{:S(2)}) async-start(), calls=%async_computation.1 | async-start | bytes 2228224 | tf_op jit(solution)/shard_map/reduce_scatter | solution.py:141
  8.6 13.8 %collective-permute-start = (bf16[512,512]{0,1:T(8,128)(2,1)S(1)}, bf16[512,512]{0,1:T(8,128)(2,1)}, u32[]{:S(2)}, u32[]{:S(2)}) collective-permute-start(bf16[512,512]{0,1:T(8,128)(2,1)S(1)} %bitcast.106), channel_id=1, source_target_pairs={{0,1},{1,2},{2,3},{3,4},{4,5},{5,6},{6,7},{7,8},{8,9},{9,10},{10,1... | collective-permute-start | bytes 1572872 | tf_op jit(solution)/shard_map/ppermute | solution.py:16
  11.8 19.4 %collective-permute-start.1 = (bf16[512,512]{1,0:T(8,128)(2,1)}, bf16[512,512]{1,0:T(8,128)(2,1)}, u32[]{:S(2)}, u32[]{:S(2)}) collective-permute-start(bf16[512,512]{1,0:T(8,128)(2,1)} %bitcast.113), channel_id=1, source_target_pairs={{0,1},{1,2},{2,3},{3,4},{4,5},{5,6},{6,7},{7,8},{8,9},{9,10},{10,1... | collective-permute-start | bytes 1572872 | tf_op jit(solution)/shard_map/ppermute | solution.py:16
  20.7 10.6 %copy-start.4 = (bf16[1,512,512]{1,2,0:T(8,128)(2,1)}, bf16[1,512,512]{1,2,0:T(8,128)(2,1)S(1)}, u32[]{:S(2)}) copy-start(bf16[1,512,512]{1,2,0:T(8,128)(2,1)S(1)} %copy.62) | copy-start | bytes 1572868
  23.7 7.5 %copy-start.8 = (bf16[512,4,128]{2,0,1:T(8,128)(2,1)}, bf16[512,4,128]{2,0,1:T(8,128)(2,1)S(1)}, u32[]{:S(2)}) copy-start(bf16[512,4,128]{2,0,1:T(8,128)(2,1)S(1)} %copy.33) | copy-start | bytes 1572868
  23.8 9.6 %copy-start.7 = (bf16[1,512,512]{1,2,0:T(8,128)(2,1)S(1)}, bf16[1,512,512]{1,2,0:T(8,128)(2,1)}, u32[]{:S(2)}) copy-start(bf16[1,512,512]{1,2,0:T(8,128)(2,1)} %copy.36) | copy-start | bytes 1572868
  38.9 90.8 %all-reduce.2.cloned.1.call-start = ((), (), s32[]{:S(2)}) async-start(), calls=%async_computation.2 | async-start | bytes 131072 | tf_op jit(solution)/shard_map/psum | solution.py:149
  38.9 3.4 %copy-start.1 = (bf16[4,512,1024]{1,2,0:T(8,128)(2,1)S(1)}, bf16[4,512,1024]{1,2,0:T(8,128)(2,1)}, u32[]{:S(2)}) copy-start(bf16[4,512,1024]{1,2,0:T(8,128)(2,1)} %get-tuple-element.25) | copy-start | bytes 12582916
  42.3 1.7 %copy-start.3 = (bf16[512,512]{0,1:T(8,128)(2,1)}, bf16[512,512]{0,1:T(8,128)(2,1)S(1)}, u32[]{:S(2)}) copy-start(bf16[512,512]{0,1:T(8,128)(2,1)S(1)} %get-tuple-element.18) | copy-start | bytes 1572868
  45.5 24.4 %collective-permute-start.3 = (f32[512,512]{1,0:T(8,128)}, f32[512,512]{1,0:T(8,128)}, u32[]{:S(2)}, u32[]{:S(2)}) collective-permute-start(f32[512,512]{1,0:T(8,128)} %copy.50), channel_id=1, source_target_pairs={{1,0},{2,1},{3,2},{4,3},{5,4},{6,5},{7,6},{8,7},{9,8},{10,9},{11,1... | collective-permute-start | bytes 3145736 | tf_op jit(solution)/shard_map/ppermute | solution.py:16
  46.9 7.6 %copy-start.5 = (bf16[1,512,512]{1,2,0:T(8,128)(2,1)S(1)}, bf16[1,512,512]{1,2,0:T(8,128)(2,1)}, u32[]{:S(2)}) copy-start(bf16[1,512,512]{1,2,0:T(8,128)(2,1)} %copy-done.4) | copy-start | bytes 1572868
  54.5 2.6 %copy-start.2 = (bf16[4,512,1024]{1,2,0:T(8,128)(2,1)}, bf16[4,512,1024]{1,2,0:T(8,128)(2,1)S(1)}, u32[]{:S(2)}) copy-start(bf16[4,512,1024]{1,2,0:T(8,128)(2,1)S(1)} %fusion.10) | copy-start | bytes 12582916
  58.4 50.1 %collective-permute-start.2 = (f32[512,512]{1,0:T(8,128)}, f32[512,512]{1,0:T(8,128)}, u32[]{:S(2)}, u32[]{:S(2)}) collective-permute-start(f32[512,512]{1,0:T(8,128)} %copy.47), channel_id=1, source_target_pairs={{1,0},{2,1},{3,2},{4,3},{5,4},{6,5},{7,6},{8,7},{9,8},{10,9},{11,1... | collective-permute-start | bytes 3145736 | tf_op jit(solution)/shard_map/ppermute | solution.py:16
Sparse Core Ops, SparseCore 0:
  39.0 67.8 reduce-scatter.1
  109.7 19.8 all-reduce.1
where the time goes:
time: 139 us; the launch traced here: 138 us
  waiting for transfers between devices  53.9 us (39%)
  matrix products  29.4 us (21%)
  local copies, waits for them, and re-layouts  19.3 us (14%)
  between operations  14.3 us (10%)
  starting transfers between devices  10.6 us (8%)
  other arithmetic  10.5 us (8%)
    reduce_scatter x1, waiting for transfers between devices, shards(): lax.psum_scatter(lax.dot_general(hidden, grad_loc, (((0,), (0,)), ((), ()...  34.9 us
    psum x1, waiting for transfers between devices, shards(): lax.psum(weight_part.astype(jnp.bfloat16), 'dp').astype(jnp.float32)  19 us
    ppermute x4, starting transfers between devices, shifted(): lax.ppermute(value, axis, [(source, source + steps) for source in range(f...  10.5 us
    unnamed x25, local copies, waits for them, and re-layouts  7.78 us
    dot_general x1, matrix products, back_piece(): jnp.einsum('rhd,chd->hrc', split_heads(d_attn), split_heads(value_piece),...  7.53 us
    dot_general x1, matrix products, score_block(): jnp.einsum('rhd,chd->hrc', split_heads(query_rows), split_heads(key_piece...  7.48 us
    dot_general x1, matrix products, back_piece(): jnp.einsum('hrc,chd->rhd', d_scores, split_heads(key_piece), preferred_el...  4.12 us
    slice x4, local copies, waits for them, and re-layouts, shards(): remote_parts = [(key_part[0:tail], value_part[0:tail])]  4.07 us
  transfers between devices with their start and end apart: 6, of which 2 were waited for; matrix products, arithmetic and copies ran while one was open for 35% of the time, Pallas kernels for 0%

commit v1 on v0

--- a/solution.py
+++ b/solution.py
@@ -146,7 +146,9 @@
         scatter_dimension=0,
         tiled=True,
     )
-    weight_total = lax.psum(weight_part.astype(jnp.bfloat16), "dp").astype(jnp.float32)
+    weight_total = jnp.sum(lax.all_gather(weight_part.astype(jnp.bfloat16), "dp"), axis=0).astype(
+        jnp.float32
+    )
     total_rows = lax.axis_size("dp") * hist_size * ev_rows
     weight_grad = weight_total / math.sqrt(total_rows)
     return (

time: 139 us -> 121 us (0.87)
  waiting for transfers between devices: 53.9 us -> 32.8 us
  blocking collectives: 0 us -> 4.93 us
  other arithmetic: 10.5 us -> 9.03 us
    psum x1 -> x0, waiting for transfers between devices: 19 us -> none  [shards(): lax.psum(weight_part.astype(jnp.bfloat16), 'dp').astype(jnp.float32)]
    all_gather x0 -> x1, blocking collectives: none -> 4.93 us  [shards(): lax.all_gather(weight_part.astype(jnp.bfloat16), 'dp')]
    reduce_scatter x1, waiting for transfers between devices: 34.9 us -> 32.7 us  [shards(): lax.psum_scatter(lax.dot_general(hidden, grad_loc, (((0,), (0,)), ((), ()...]
  transfers between devices with their start and end apart: 6 -> 5, of which waited for: 2 -> 1; matrix products, arithmetic and copies ran while one was open for 35% -> 39% of each run, Pallas kernels for 0% -> 0%
where the time goes in v1:
time: 121 us; the launch traced here: 120 us
  waiting for transfers between devices  32.8 us (27%)
  matrix products  29.4 us (24%)
  local copies, waits for them, and re-layouts  19.3 us (16%)
  between operations  14.3 us (12%)
  starting transfers between devices  10.5 us (9%)
  other arithmetic  9.03 us (7%)
  blocking collectives  4.93 us (4%)
    reduce_scatter x1, waiting for transfers between devices, shards(): lax.psum_scatter(lax.dot_general(hidden, grad_loc, (((0,), (0,)), ((), ()...  32.7 us
    ppermute x4, starting transfers between devices, shifted(): lax.ppermute(value, axis, [(source, source + steps) for source in range(f...  10.5 us
    unnamed x25, local copies, waits for them, and re-layouts  7.78 us
    dot_general x1, matrix products, back_piece(): jnp.einsum('rhd,chd->hrc', split_heads(d_attn), split_heads(value_piece),...  7.53 us
    dot_general x1, matrix products, score_block(): jnp.einsum('rhd,chd->hrc', split_heads(query_rows), split_heads(key_piece...  7.49 us
    all_gather x1, blocking collectives, shards(): lax.all_gather(weight_part.astype(jnp.bfloat16), 'dp')  4.93 us
    dot_general x1, matrix products, back_piece(): jnp.einsum('hrc,chd->rhd', d_scores, split_heads(key_piece), preferred_el...  4.12 us
    slice x4, local copies, waits for them, and re-layouts, shards(): remote_parts = [(key_part[0:tail], value_part[0:tail])]  4.05 us
  transfers between devices with their start and end apart: 5, of which 1 were waited for; matrix products, arithmetic and copies ran while one was open for 39% of the time, Pallas kernels for 0%

profile of v1, /device:TPU:0, one launch (start us, length us, event | category | flops | bytes accessed | tf_op | source)
XLA Modules:
  0.0 120.3 jit_solution(11984075190738245557)
XLA Ops:
  7.2 1.4 %copy.31 = bf16[1,512,512]{1,2,0:T(8,128)(2,1)S(1)} copy(bf16[1,512,512]{2,1,0:T(8,128)(2,1)} %param.8) | data formatting | bytes 1048576 | tf_op args[1]
  8.6 3.2 %collective-permute-start = (bf16[512,512]{0,1:T(8,128)(2,1)S(1)}, bf16[512,512]{0,1:T(8,128)(2,1)}, u32[]{:S(2)}, u32[]{:S(2)}) collective-permute-start(bf16[512,512]{0,1:T(8,128)(2,1)S(1)} %bitcast.107), channel_id=1, source_target_pairs={{0,1},{1,2},{2,3},{3,4},{4,5},{5,6},{6,7},{7,8},{8,9},{9,10},{10,1... | collective-permute-start | bytes 1572872 | tf_op jit(solution)/shard_map/ppermute | solution.py:16
  11.8 4.5 %collective-permute-start.1 = (bf16[512,512]{1,0:T(8,128)(2,1)}, bf16[512,512]{1,0:T(8,128)(2,1)}, u32[]{:S(2)}, u32[]{:S(2)}) collective-permute-start(bf16[512,512]{1,0:T(8,128)(2,1)} %bitcast.115), channel_id=1, source_target_pairs={{0,1},{1,2},{2,3},{3,4},{4,5},{5,6},{6,7},{7,8},{8,9},{9,10},{10,1... | collective-permute-start | bytes 1572872 | tf_op jit(solution)/shard_map/ppermute | solution.py:16
  16.4 2.0 %copy.36 = bf16[1,512,512]{1,2,0:T(8,128)(2,1)} copy(bf16[1,512,512]{2,1,0:T(8,128)(2,1)} %param.9) | data formatting | bytes 1048576 | tf_op args[2]
  18.4 1.0 copy.34
  19.4 1.3 %copy.62 = bf16[1,512,512]{1,2,0:T(8,128)(2,1)S(1)} copy(bf16[1,512,512]{2,1,0:T(8,128)(2,1)} %param.7) | data formatting | bytes 1048576 | tf_op jit(solution)/shard_map/reshape;squeeze | solution.py:20
  20.9 0.7 fusion.18
  21.6 0.8 pad_add_fusion
  22.4 1.3 %copy.33 = bf16[512,4,128]{2,0,1:T(8,128)(2,1)S(1)} copy(bf16[512,4,128]{0,2,1:T(8,128)(2,1)} %bitcast.1) | data formatting | bytes 1048576 | tf_op jit(solution)/shard_map/concatenate | solution.py:123
  23.8 7.5 %fusion.5 = (bf16[4,512,1024]{1,2,0:T(8,128)(2,1)}, f32[4,1024,512]{2,1,0:T(8,128)}) fusion(pred[512,1024]{0,1:T(8,128)(4,1)} %pad_add_fusion, bf16[512,4,128]{0,2,1:T(8,128)(2,1)S(1)} %bitcast.112, bf16[512,4,128]{2,0,1:T(8,128)(2,1)} %copy.34, bf16[512,4,128]{2,0,1:T(8,128)(2,1)S(1)} %copy.33), kind=kOutput, calls=%fused_computation.8 | convolution fusion | flops 555745280 | bytes 14680064 | tf_op jit(solution)/shard_map/rhd,chd->hrc/dot_general | solution.py:24
  31.3 2.0 %copy.35 = bf16[512,512]{0,1:T(8,128)(2,1)} copy(bf16[512,512]{1,0:T(8,128)(2,1)} %collective-permute-done.1) | data formatting | bytes 1048576 | tf_op jit(solution)/shard_map/ppermute | solution.py:16
  33.3 3.1 %fusion.32 = (f32[512]{0:T(512)S(1)}, f32[4,128,512]{2,1,0:T(8,128)S(1)}) fusion(bf16[4,512,1024]{1,2,0:T(8,128)(2,1)} %get-tuple-element.25, bf16[512,4,128]{0,2,1:T(8,128)(2,1)S(1)} %bitcast.117, bf16[512,4,128]{0,2,1:T(8,128)(2,1)} %bitcast.118), kind=kOutput, calls=%fused_computation.62 | convolution fusion | flops 539229696 | bytes 6293504 | tf_op jit(solution)/shard_map/hrc,chd->rhd/dot_general | solution.py:47
  36.8 2.0 %fusion.13 = f32[512,1024]{1,0:T(8,128)} fusion(bf16[512,512]{0,1:T(8,128)(2,1)S(1)} %bitcast.109, bf16[1,512,1024]{2,1,0:T(8,128)(2,1)S(1)} %copy-done), kind=kOutput, calls=%fused_computation.28 | convolution fusion | flops 536870912 | bytes 3670016 | tf_op jit(solution)/shard_map/dot_general | solution.py:142
  38.9 2.2 %fusion.25 = (f32[512]{0:T(512)S(1)}, f32[512]{0:T(512)S(1)}, f32[512,512]{0,1:T(8,128)S(1)}) fusion(bf16[1,512,512]{1,2,0:T(8,128)(2,1)S(1)} %copy.39, f32[512]{0:T(512)S(1)} %add_rsqrt_fusion, f32[512]{0:T(512)S(1)} %broadcast_multiply_fusion.2, f32[4,128,512]{2,1,0:T(8,128)S(1)} %get-tuple-element.28, bf16[512,1024]{1,0:T(8,128)(2,1)} %param.12, ...), kind=kOutput, calls=%fused_computation.48 | convolution fusion | flops 538704896 | bytes 4726784 | tf_op jit(solution)/shard_map/dot_general | solution.py:90
  41.1 1.2 multiply_convert_fusion.1
  42.3 1.5 %convolution_bitcast_fusion = f32[1024,4,128]{0,2,1:T(8,128)S(1)} fusion(bf16[512,4,128]{0,2,1:T(8,128)(2,1)S(1)} %bitcast.110, bf16[4,512,1024]{1,2,0:T(8,128)(2,1)S(1)} %copy-done.1), kind=kOutput, calls=%fused_computation.16 | convolution fusion | flops 536870912 | bytes 6815744 | tf_op jit(solution)/shard_map/hrc,rhd->chd/dot_general | solution.py:75
  44.0 1.4 %copy.50 = f32[512,512]{1,0:T(8,128)} copy(f32[512,512]{0,1:T(8,128)S(1)} %bitcast.104) | data formatting | bytes 2097152 | tf_op jit(solution)/shard_map/slice | solution.py:134
  45.4 1.5 %collective-permute-start.3 = (f32[512,512]{1,0:T(8,128)}, f32[512,512]{1,0:T(8,128)}, u32[]{:S(2)}, u32[]{:S(2)}) collective-permute-start(f32[512,512]{1,0:T(8,128)} %copy.50), channel_id=1, source_target_pairs={{1,0},{2,1},{3,2},{4,3},{5,4},{6,5},{7,6},{8,7},{9,8},{10,9},{11,1... | collective-permute-start | bytes 3145736 | tf_op jit(solution)/shard_map/ppermute | solution.py:16
  46.9 7.5 %fusion.10 = bf16[4,512,1024]{1,2,0:T(8,128)(2,1)S(1)} fusion(f32[4,1024,512]{2,1,0:T(8,128)} %get-tuple-element.26, pred[512,1024]{0,1:T(8,128)(4,1)} %pad_add_fusion, bf16[512,4,128]{0,2,1:T(8,128)(2,1)} %bitcast.111, bf16[512,4,128]{0,2,1:T(8,128)(2,1)} %bitcast.116, bf16[512,4,128]{0,2,1:T(8,128)(2,1)} %bitcast.119), kind=kOutput, calls=%fused_computation.13 | convolution fusion | flops 564133888 | bytes 14680064 | tf_op jit(solution)/shard_map/rhd,chd->hrc/dot_general | solution.py:57
  54.4 1.5 %multiply_bitcast_fusion = f32[1024,4,128]{0,2,1:T(8,128)S(1)} fusion(bf16[4,512,1024]{1,2,0:T(8,128)(2,1)S(1)} %fusion.10, bf16[512,4,128]{0,2,1:T(8,128)(2,1)S(1)} %bitcast.113), kind=kOutput, calls=%fused_computation.14 | convolution fusion | flops 537395200 | bytes 6815744 | tf_op jit(solution)/shard_map/hrc,rhd->chd/dot_general | solution.py:72
  55.9 1.1 fusion.31
  57.1 1.3 %copy.47 = f32[512,512]{1,0:T(8,128)} copy(f32[512,512]{0,1:T(8,128)S(1)} %bitcast.105) | data formatting | bytes 2097152 | tf_op jit(solution)/shard_map/slice | solution.py:134
  58.4 1.3 %collective-permute-start.2 = (f32[512,512]{1,0:T(8,128)}, f32[512,512]{1,0:T(8,128)}, u32[]{:S(2)}, u32[]{:S(2)}) collective-permute-start(f32[512,512]{1,0:T(8,128)} %copy.47), channel_id=1, source_target_pairs={{1,0},{2,1},{3,2},{4,3},{5,4},{6,5},{7,6},{8,7},{9,8},{10,9},{11,1... | collective-permute-start | bytes 3145736 | tf_op jit(solution)/shard_map/ppermute | solution.py:16
  60.0 1.6 %copy.48 = f32[512,512]{1,0:T(8,128)S(1)} copy(f32[512,512]{0,1:T(8,128)} %bitcast.103) | data formatting | bytes 2097152 | tf_op jit(solution)/shard_map/slice | solution.py:132
  61.6 4.1 %fusion.11 = bf16[4,128,512]{2,1,0:T(8,128)(2,1)} fusion(bf16[4,512,1024]{1,2,0:T(8,128)(2,1)} %copy-done.2, bf16[512,4,128]{2,0,1:T(8,128)(2,1)} %copy.34, bf16[512,4,128]{2,0,1:T(8,128)(2,1)} %copy-done.8), kind=kOutput, calls=%fused_computation.22 | convolution fusion | flops 539492352 | bytes 5767168 | tf_op jit(solution)/shard_map/hrc,chd->rhd/dot_general | solution.py:68
  65.7 2.1 %copy.52 = bf16[1,512,512]{2,1,0:T(8,128)(2,1)} copy(bf16[1,512,512]{1,2,0:T(8,128)(2,1)} %bitcast.120) | data formatting | bytes 1048576
  67.8 2.0 %copy.53 = bf16[1,512,512]{2,1,0:T(8,128)(2,1)} copy(bf16[1,512,512]{1,2,0:T(8,128)(2,1)} %bitcast.106) | data formatting | bytes 1048576
  69.8 2.2 %fusion.24 = bf16[1,512,512]{2,1,0:T(8,128)(2,1)} fusion(f32[512,512]{1,0:T(8,128)S(1)} %copy.51, f32[512,512]{1,0:T(8,128)} %collective-permute-done.3), kind=kLoop, calls=%fused_computation.47 | loop fusion | flops 524288 | bytes 2621440 | tf_op jit(solution)/shard_map/broadcast_in_dim | solution.py:157
  72.0 2.2 %fusion.23 = bf16[1,512,512]{2,1,0:T(8,128)(2,1)} fusion(f32[512,512]{1,0:T(8,128)S(1)} %copy.48, f32[512,512]{1,0:T(8,128)} %collective-permute-done.2), kind=kLoop, calls=%fused_computation.46 | loop fusion | flops 524288 | bytes 2621440 | tf_op jit(solution)/shard_map/broadcast_in_dim | solution.py:156
  74.2 32.7 %reduce-scatter.2.cloned.1.call-done = f32[32,1024]{1,0:T(8,128)} async-done(((f32[512,1024]{1,0:T(8,128)}), f32[32,1024]{1,0:T(8,128)}) %reduce-scatter.2.cloned.1.call-update) | async-done | bytes 131088 | tf_op jit(solution)/shard_map/reduce_scatter | solution.py:141
  106.9 0.9 convert_element_type.76
  107.8 4.9 %all-gather = bf16[64,1024]{1,0:T(8,128)(2,1)S(1)} all-gather(bf16[32,1024]{1,0:T(8,128)(2,1)S(1)} %convert_element_type.76), channel_id=2, replica_groups=mesh['dp'=2,'hist'=16] {'dp'}, dimensions={0}, use_global_device_ids=true | all-gather | bytes 196608 | tf_op jit(solution)/shard_map/all_gather | solution.py:149
  (38 shorter events, 1.9 us)
Async XLA Ops:
  7.2 29.7 %copy-start = (bf16[1,512,1024]{2,1,0:T(8,128)(2,1)S(1)}, bf16[1,512,1024]{2,1,0:T(8,128)(2,1)}, u32[]{:S(2)}) copy-start(bf16[1,512,1024]{2,1,0:T(8,128)(2,1)} %param.13) | copy-start | bytes 3145732
  7.2 13.5 %copy-start.6 = (bf16[1,512,512]{2,1,0:T(8,128)(2,1)S(1)}, bf16[1,512,512]{2,1,0:T(8,128)(2,1)}, u32[]{:S(2)}) copy-start(bf16[1,512,512]{2,1,0:T(8,128)(2,1)} %param.10) | copy-start | bytes 1572868
  7.2 13.7 %copy-start.9 = (s32[1,512]{1,0:T(1,128)S(1)}, s32[1,512]{1,0:T(1,128)}, u32[]{:S(2)}) copy-start(s32[1,512]{1,0:T(1,128)} %param.11) | copy-start | bytes 6148
  7.2 99.7 %reduce-scatter.2.cloned.1.call-start = ((), (), s32[]{:S(2)}) async-start(), calls=%async_computation.1 | async-start | bytes 2228224 | tf_op jit(solution)/shard_map/reduce_scatter | solution.py:141
  8.6 13.8 %collective-permute-start = (bf16[512,512]{0,1:T(8,128)(2,1)S(1)}, bf16[512,512]{0,1:T(8,128)(2,1)}, u32[]{:S(2)}, u32[]{:S(2)}) collective-permute-start(bf16[512,512]{0,1:T(8,128)(2,1)S(1)} %bitcast.107), channel_id=1, source_target_pairs={{0,1},{1,2},{2,3},{3,4},{4,5},{5,6},{6,7},{7,8},{8,9},{9,10},{10,1... | collective-permute-start | bytes 1572872 | tf_op jit(solution)/shard_map/ppermute | solution.py:16
  11.8 19.5 %collective-permute-start.1 = (bf16[512,512]{1,0:T(8,128)(2,1)}, bf16[512,512]{1,0:T(8,128)(2,1)}, u32[]{:S(2)}, u32[]{:S(2)}) collective-permute-start(bf16[512,512]{1,0:T(8,128)(2,1)} %bitcast.115), channel_id=1, source_target_pairs={{0,1},{1,2},{2,3},{3,4},{4,5},{5,6},{6,7},{7,8},{8,9},{9,10},{10,1... | collective-permute-start | bytes 1572872 | tf_op jit(solution)/shard_map/ppermute | solution.py:16
  20.7 10.6 %copy-start.4 = (bf16[1,512,512]{1,2,0:T(8,128)(2,1)}, bf16[1,512,512]{1,2,0:T(8,128)(2,1)S(1)}, u32[]{:S(2)}) copy-start(bf16[1,512,512]{1,2,0:T(8,128)(2,1)S(1)} %copy.62) | copy-start | bytes 1572868
  23.7 7.5 %copy-start.8 = (bf16[512,4,128]{2,0,1:T(8,128)(2,1)}, bf16[512,4,128]{2,0,1:T(8,128)(2,1)S(1)}, u32[]{:S(2)}) copy-start(bf16[512,4,128]{2,0,1:T(8,128)(2,1)S(1)} %copy.33) | copy-start | bytes 1572868
  23.8 9.6 %copy-start.7 = (bf16[1,512,512]{1,2,0:T(8,128)(2,1)S(1)}, bf16[1,512,512]{1,2,0:T(8,128)(2,1)}, u32[]{:S(2)}) copy-start(bf16[1,512,512]{1,2,0:T(8,128)(2,1)} %copy.36) | copy-start | bytes 1572868
  38.9 3.4 %copy-start.1 = (bf16[4,512,1024]{1,2,0:T(8,128)(2,1)S(1)}, bf16[4,512,1024]{1,2,0:T(8,128)(2,1)}, u32[]{:S(2)}) copy-start(bf16[4,512,1024]{1,2,0:T(8,128)(2,1)} %get-tuple-element.25) | copy-start | bytes 12582916
  42.3 1.7 %copy-start.3 = (bf16[512,512]{0,1:T(8,128)(2,1)}, bf16[512,512]{0,1:T(8,128)(2,1)S(1)}, u32[]{:S(2)}) copy-start(bf16[512,512]{0,1:T(8,128)(2,1)S(1)} %get-tuple-element.18) | copy-start | bytes 1572868
  45.4 24.4 %collective-permute-start.3 = (f32[512,512]{1,0:T(8,128)}, f32[512,512]{1,0:T(8,128)}, u32[]{:S(2)}, u32[]{:S(2)}) collective-permute-start(f32[512,512]{1,0:T(8,128)} %copy.50), channel_id=1, source_target_pairs={{1,0},{2,1},{3,2},{4,3},{5,4},{6,5},{7,6},{8,7},{9,8},{10,9},{11,1... | collective-permute-start | bytes 3145736 | tf_op jit(solution)/shard_map/ppermute | solution.py:16
  46.9 7.6 %copy-start.5 = (bf16[1,512,512]{1,2,0:T(8,128)(2,1)S(1)}, bf16[1,512,512]{1,2,0:T(8,128)(2,1)}, u32[]{:S(2)}) copy-start(bf16[1,512,512]{1,2,0:T(8,128)(2,1)} %copy-done.4) | copy-start | bytes 1572868
  54.4 2.6 %copy-start.2 = (bf16[4,512,1024]{1,2,0:T(8,128)(2,1)}, bf16[4,512,1024]{1,2,0:T(8,128)(2,1)S(1)}, u32[]{:S(2)}) copy-start(bf16[4,512,1024]{1,2,0:T(8,128)(2,1)S(1)} %fusion.10) | copy-start | bytes 12582916
  58.4 13.6 %collective-permute-start.2 = (f32[512,512]{1,0:T(8,128)}, f32[512,512]{1,0:T(8,128)}, u32[]{:S(2)}, u32[]{:S(2)}) collective-permute-start(f32[512,512]{1,0:T(8,128)} %copy.47), channel_id=1, source_target_pairs={{1,0},{2,1},{3,2},{4,3},{5,4},{6,5},{7,6},{8,7},{9,8},{10,9},{11,1... | collective-permute-start | bytes 3145736 | tf_op jit(solution)/shard_map/ppermute | solution.py:16
Sparse Core Ops, SparseCore 0:
  39.0 67.8 reduce-scatter.1
